TPU v7x, 512 devices: a whole 4x4x16 slice. The times are simulated.
512 devices in a mesh: row: 16 (over y, x), col: 16 (over z), depth: 2 (over core).
Axes of the slice: x: 4, y: 4, z: 16, core: 2. Of those that a mesh axis runs over, the one named last changes fastest.
Arguments:
- left_store: float32 [16, 2, 16, 2, 64, 1024], P('row', 'depth', 'col'), may hold values from -6 to 6
- left_home: int32 [16, 2, 16], P('row', 'depth'), may hold values from 0 to 15, each once within a row
- up_store: float32 [16, 2, 16, 2, 64, 1024], P('col', 'depth', 'row'), may hold values from -0.3125 to 0.3125
- up_home: int32 [16, 2, 16], P('col', 'depth'), may hold values from 0 to 15, each once within a row
- targets: int32 [16, 16, 2], P('row', 'col'), may hold values from 0 to 63, as said below
- sketch: float32 [16, 16, 2, 64, 1024], P('row', 'col'), may hold values from -0.1875 to 0.1875
Outputs:
- basis: float32 [16, 16, 2, 64, 1024], P('row', 'col', 'depth')
- weights: float32 [16, 16, 2, 64, 1024], P('row', 'col', 'depth')
Inputs may be any that keep to these rules, and one draw needn't show every extreme that they name: `left_home`: for each row and depth index the entries are the store positions 0 to 15, each once. `up_home`: for each col and depth index the entries are the store positions 0 to 15, each once. `targets`: the 2 entries of one row and col index are distinct.
All inputs are finite; a program needn't handle non-finite values.
Results may differ from a plain program's by a relative error of at most 0.0003.
Values sent between devices are 32-bit elements; how exact they have to be, the bound alone decides.
No kernel may reach another device: no remote copies, remote signals or barrier semaphores. Data moves between devices by JAX's collectives and lax.ppermute only.
A program may use at most 128 MiB of HBM per device.

v0:
```python
import math
import jax
import jax.numpy as jnp
from jax import lax
from jax.sharding import PartitionSpec as P

KD = 2
RB = 8
CB = 8


def split_up(shard, dim, devices):
    before, after = (shard.shape[:dim], shard.shape[dim + 1 :])
    return jnp.moveaxis(shard.reshape(*before, devices, -1, *after), dim, 0)


def sent_and_summed(shard, axis, dim):
    devices = lax.axis_size(axis)
    pieces = lax.all_to_all(split_up(shard, dim, devices), axis, 0, 0, tiled=True)
    return jnp.sum(pieces, axis=0)


def laid_out(pieces, dim):
    pieces = jnp.moveaxis(pieces, 0, dim)
    shape = pieces.shape
    return pieces.reshape(*shape[:dim], shape[dim] * shape[dim + 1], *shape[dim + 2 :])


def copy_for_each(shard, axis):
    devices = lax.axis_size(axis)
    return lax.all_to_all(
        jnp.broadcast_to(shard[None], (devices, *shard.shape)), axis, 0, 0, tiled=True
    )


def gathered_copies(shard, axis, dim):
    return laid_out(copy_for_each(shard, axis), dim)


def orthonormal(sample):
    gram_mat = jnp.einsum("pat,pbt->pab", sample, sample, precision=lax.Precision.HIGHEST)
    factor_low = jnp.linalg.cholesky(gram_mat)
    return lax.linalg.triangular_solve(factor_low, sample, left_side=True, lower=True)


def shards(left_store, left_home, up_store, up_home, targets, sketch):
    high = lax.Precision.HIGHEST
    left_local = left_store[0, 0]
    up_local = up_store[0, 0]
    left_table = left_home[0, 0]
    up_table = up_home[0, 0]
    left_all = lax.all_gather(left_local, "col", axis=0, tiled=True)
    up_all = lax.all_gather(up_local, "row", axis=0, tiled=True)
    left_pairs = jnp.take(left_all, left_table, axis=0)
    up_pairs = jnp.take(up_all, up_table, axis=0)
    chosen = targets[0, 0]
    block_row = chosen // CB
    block_col = chosen % CB
    row_pairs = jnp.take(left_pairs.reshape((RB, KD) + left_local.shape[1:]), block_row, axis=0)
    col_pairs = jnp.take(up_pairs.reshape((CB, KD) + up_local.shape[1:]), block_col, axis=0)
    row_basis = row_pairs[:, :, 0]
    row_coef = row_pairs[:, :, 1]
    col_coef = col_pairs[:, :, 0]
    col_basis = col_pairs[:, :, 1]
    test_rows = sketch[0, 0]
    middle = jnp.einsum("pkat,pkbt->pkab", row_coef, col_coef, precision=high)
    test_side = jnp.einsum("pat,pkbt->pkab", test_rows, col_basis, precision=high)
    folded = jnp.einsum("pkab,pkcb->pkac", test_side, middle, precision=high)
    sample_part = jnp.einsum("pkac,pkct->pat", folded, row_basis, precision=high)
    own_sketch = sent_and_summed(sample_part, "depth", 0)
    own_basis = orthonormal(own_sketch)
    bases = gathered_copies(own_basis, "depth", 0)
    inner_prod = jnp.einsum("pat,pkct->pkac", bases, row_basis, precision=high)
    turned = jnp.einsum("pkac,pkcb->pkab", inner_prod, middle, precision=high)
    project_part = jnp.einsum("pkab,pkbt->pat", turned, col_basis, precision=high)
    projected = sent_and_summed(project_part, "depth", 0)
    root_tile = math.sqrt(test_rows.shape[-1])
    return ((own_basis * root_tile)[None, None], (projected / root_tile)[None, None])


def solution(mesh):
    return jax.shard_map(
        shards,
        mesh=mesh,
        in_specs=(
            P("row", "depth", "col", None, None, None),
            P("row", "depth", None),
            P("col", "depth", "row", None, None, None),
            P("col", "depth", None),
            P("row", "col", None),
            P("row", "col", None, None, None),
        ),
        out_specs=(P("row", "col", "depth", None, None), P("row", "col", "depth", None, None)),
        check_vma=False,
    )
```

profile of v0, /device:TPU:1, one launch (start us, length us, event | category | flops | bytes accessed | tf_op | source)
XLA Modules:
  0.0 273.3 jit_solution(12288357249461976770)
XLA Ops:
  7.2 0.0 copy-start
  7.2 0.0 all-gather.7.cloned.1.call-start
  7.2 0.7 all-gather.7.cloned.1.call-update
  7.9 0.0 all-gather.5.cloned.1.call-start
  8.0 0.7 all-gather.5.cloned.1.call-update
  8.7 0.7 compare_select_fusion.1
  9.3 0.7 compare_and_fusion
  10.0 0.7 compare_select_fusion.3
  10.7 0.7 compare_and_fusion.1
  11.4 0.7 compare_and_fusion.3
  12.0 109.1 %all-gather.7.cloned.1.call-done = f32[16,1,1,2,64,1024]{5,4,3,2,1,0:T(8,128)} async-done(((f32[1,1,1,2,64,1024]{5,4,3,2,1,0:T(8,128)}), f32[16,1,1,2,64,1024]{5,4,3,2,1,0:T(8,128)}) %all-gather.7.cloned.1.call-update) | async-done | bytes 8388624 | tf_op jit(solution)/shard_map/all_gather | solution.py:52
  121.1 7.7 %gather_fusion.2 = f32[16,2,64,1024]{3,2,1,0:T(8,128)} fusion(f32[16,2,64,1024]{3,2,1,0:T(8,128)} %bitcast.97, s32[1024]{0:T(1024)S(1)} %pad_clamp_fusion.1), kind=kCustom, calls=%fused_computation.2.clone | custom fusion | bytes 16777280 | tf_op jit(solution)/shard_map/jit(_take)/gather | solution.py:54
  128.8 8.6 %broadcast_select_fusion = f32[16,2,64,1024]{3,2,1,0:T(8,128)} fusion(f32[16,2,64,1024]{3,2,1,0:T(8,128)} %gather_fusion.2, pred[16]{0:T(512)(128)(4,1)S(1)} %compare_and_fusion.1), kind=kLoop, calls=%fused_computation.4 | loop fusion | flops 2097152 | bytes 16777232 | tf_op jit(solution)/shard_map/jit(_take)/select_n | solution.py:54
  137.4 5.8 %gather_fusion.3 = f32[2,2,2,64,1024]{4,3,2,1,0:T(8,128)} fusion(f32[8,2,2,64,1024]{4,3,2,1,0:T(8,128)} %bitcast.94, s32[1024]{0:T(1024)S(1)} %pad_clamp_fusion), kind=kCustom, calls=%fused_computation.3.clone | custom fusion | bytes 4194312 | tf_op jit(solution)/shard_map/jit(_take)/gather | solution.py:59
  143.2 65.0 %all-gather.5.cloned.1.call-done = f32[16,1,1,2,64,1024]{5,4,3,2,1,0:T(8,128)} async-done(((f32[1,1,1,2,64,1024]{5,4,3,2,1,0:T(8,128)}), f32[16,1,1,2,64,1024]{5,4,3,2,1,0:T(8,128)}) %all-gather.5.cloned.1.call-update) | async-done | bytes 8388624 | tf_op jit(solution)/shard_map/all_gather | solution.py:53
  208.2 7.7 %gather_fusion = f32[16,2,64,1024]{3,2,1,0:T(8,128)} fusion(f32[16,2,64,1024]{3,2,1,0:T(8,128)} %bitcast.96, s32[1024]{0:T(1024)S(1)} %pad_clamp_fusion.3), kind=kCustom, calls=%fused_computation.clone | custom fusion | bytes 16777280 | tf_op jit(solution)/shard_map/jit(_take)/gather | solution.py:55
  215.8 8.6 %broadcast_select_fusion.1 = f32[16,2,64,1024]{3,2,1,0:T(8,128)} fusion(f32[16,2,64,1024]{3,2,1,0:T(8,128)} %gather_fusion, pred[16]{0:T(512)(128)(4,1)S(1)} %compare_and_fusion.3), kind=kLoop, calls=%fused_computation.5 | loop fusion | flops 2097152 | bytes 16777232 | tf_op jit(solution)/shard_map/jit(_take)/select_n | solution.py:55
  224.4 5.4 %gather_fusion.1 = f32[2,2,2,64,1024]{4,3,2,1,0:T(8,128)} fusion(f32[8,2,2,64,1024]{4,3,2,1,0:T(8,128)} %bitcast.95, s32[1024]{0:T(1024)S(1)} %pad_clamp_fusion.2), kind=kCustom, calls=%fused_computation.1.clone | custom fusion | bytes 4194312 | tf_op jit(solution)/shard_map/jit(_take)/gather | solution.py:60
  229.9 2.8 %copy_select_fusion = (f32[2,2,2,64,1024]{4,3,1,0,2:T(8,128)S(1)}, f32[2,2,2,64,1024]{4,3,1,0,2:T(8,128)S(1)}) fusion(f32[2,2,2,64,1024]{4,3,2,1,0:T(8,128)} %gather_fusion.3, pred[2]{0:T(512)(128)(4,1)S(1)} %get-tuple-element.4, f32[2,2,2,64,1024]{4,3,2,1,0:T(8,128)} %gather_fusion.1, pred[2]{0:T(512)(128)(4,1)S(1)} %get-tuple-element.8), kind=kLoop, calls=%fused_computation.6 | loop fusion | flops 1048576 | bytes 8388612 | tf_op jit(solution)/shard_map/jit(_take)/select_n | solution.py:59
  232.6 0.0 copy-start.1
  232.6 0.0 copy-done
  232.7 1.6 fusion.1
  234.3 1.1 fusion
  235.4 0.3 fusion.9
  235.7 0.0 copy-done.1
  235.7 0.7 convolution_bitcast_fusion.1
  236.4 4.6 %all_to_all.15 = f32[2,1,64,1024]{3,2,1,0:T(8,128)S(1)} all-to-all(f32[2,1,64,1024]{3,2,1,0:T(8,128)S(1)} %convolution_bitcast_fusion.1), channel_id=1, replica_groups=mesh['row'=16,'col'=16,'depth'=2] {'depth'}, dimensions={0} | all-to-all | bytes 1048576 | tf_op jit(solution)/shard_map/all_to_all | solution.py:19
  241.1 0.4 fusion.10
  241.4 0.1 copy.27
  241.5 5.8 %custom-call.7 = f32[1,64,64]{2,1,0:T(8,128)S(1)} custom-call(f32[1,64,64]{2,1,0:T(8,128)S(1)} %fusion.6), custom_call_target="Cholesky" | custom-call | tf_op jit(solution)/shard_map/jit(cholesky)/cholesky | solution.py:42
  247.4 0.6 compare_reduce_fusion
  248.1 0.7 fusion.5
  248.7 4.9 %custom-call.8 = f32[1,1,64,64]{2,3,1,0:T(8,128)S(1)} custom-call(f32[1,1,64,64]{3,2,1,0:T(8,128)S(1)} %fusion.5), custom_call_target="InvertDiagBlocksLowerTriangular" | custom-call | tf_op jit(solution)/shard_map/triangular_solve | solution.py:43
  253.6 0.0 copy-start.2
  253.6 0.4 fusion.7
  254.1 0.7 multiply_bitcast_fusion.1
  254.8 4.2 %all_to_all.16 = f32[2,1,64,1024]{3,2,1,0:T(8,128)S(1)} all-to-all(f32[2,1,64,1024]{3,2,1,0:T(8,128)S(1)} %broadcast_in_dim.33), channel_id=1, replica_groups=mesh['row'=16,'col'=16,'depth'=2] {'depth'}, dimensions={0} | all-to-all | bytes 1048576 | tf_op jit(solution)/shard_map/all_to_all | solution.py:31
  259.0 0.0 copy-done.2
  259.0 1.6 fusion.2
  260.6 0.3 fusion.11
  260.9 0.7 convolution_bitcast_fusion
  261.6 4.2 %all_to_all.17 = f32[2,1,64,1024]{3,2,1,0:T(8,128)S(1)} all-to-all(f32[2,1,64,1024]{3,2,1,0:T(8,128)S(1)} %convolution_bitcast_fusion), channel_id=1, replica_groups=mesh['row'=16,'col'=16,'depth'=2] {'depth'}, dimensions={0} | all-to-all | bytes 1048576 | tf_op jit(solution)/shard_map/all_to_all | solution.py:19
  265.8 0.7 multiply_bitcast_fusion
  (9 shorter events, 0.2 us)
Async XLA Ops:
  7.2 225.5 %copy-start = (f32[1,1,2,64,1024]{4,3,2,1,0:T(8,128)S(1)}, f32[1,1,2,64,1024]{4,3,2,1,0:T(8,128)}, u32[]{:S(2)}) copy-start(f32[1,1,2,64,1024]{4,3,2,1,0:T(8,128)} %param.15) | copy-start | bytes 1572868
  7.2 113.9 %all-gather.7.cloned.1.call-start = ((), (), s32[]{:S(2)}) async-start(), calls=%async_computation.4 | async-start | bytes 8912896 | tf_op jit(solution)/shard_map/all_gather | solution.py:52
  7.9 200.3 %all-gather.5.cloned.1.call-start = ((), (), s32[]{:S(2)}) async-start(), calls=%async_computation.3 | async-start | bytes 8912896 | tf_op jit(solution)/shard_map/all_gather | solution.py:53
  232.6 3.1 %copy-start.1 = (f32[2,2,2,64,1024]{4,3,1,0,2:T(8,128)}, f32[2,2,2,64,1024]{4,3,1,0,2:T(8,128)S(1)}, u32[]{:S(2)}) copy-start(f32[2,2,2,64,1024]{4,3,1,0,2:T(8,128)S(1)} %get-tuple-element.10) | copy-start | bytes 6291460
  253.6 5.4 %copy-start.2 = (f32[2,2,2,64,1024]{4,3,1,0,2:T(8,128)S(1)}, f32[2,2,2,64,1024]{4,3,1,0,2:T(8,128)}, u32[]{:S(2)}) copy-start(f32[2,2,2,64,1024]{4,3,1,0,2:T(8,128)} %copy-done.1) | copy-start | bytes 6291460
Sparse Core Ops, SparseCore 0:
  10.1 110.9 all-gather.6
  124.1 84.0 all-gather.4
where the time goes:
time: 274 us; the launch traced here: 273 us
  waiting for transfers between devices  175 us (64%)
  other arithmetic  36.9 us (13%)
  local copies, waits for them, and re-layouts  26.7 us (10%)
  between operations  14.2 us (5%)
  blocking collectives  12.9 us (5%)
  matrix products  7.07 us (3%)
    all_gather x1, waiting for transfers between devices, shards(): left_all = lax.all_gather(left_local, 'col', axis=0, tiled=True)  109 us
    all_gather x1, waiting for transfers between devices, shards(): up_all = lax.all_gather(up_local, 'row', axis=0, tiled=True)  65 us
    select_n x2, other arithmetic, shards(): left_pairs = jnp.take(left_all, left_table, axis=0)  9.27 us
    select_n x2, other arithmetic, shards(): up_pairs = jnp.take(up_all, up_table, axis=0)  9.26 us
    all_to_all x2, blocking collectives, sent_and_summed(): lax.all_to_all(split_up(shard, dim, devices), axis, 0, 0, tiled=True)  8.78 us
    gather x1, local copies, waits for them, and re-layouts, shards(): left_pairs = jnp.take(left_all, left_table, axis=0)  7.68 us
    gather x1, local copies, waits for them, and re-layouts, shards(): up_pairs = jnp.take(up_all, up_table, axis=0)  7.67 us
    another operation x3, other arithmetic, orthonormal(): factor_low = jnp.linalg.cholesky(gram_mat)  6.52 us
  transfers between devices with their start and end apart: 2, of which 2 were waited for; matrix products, arithmetic and copies ran while one was open for 9% of the time, Pallas kernels for 0%

commit v1 on v0

--- a/solution.py
+++ b/solution.py
@@ -7,6 +7,19 @@
 KD = 2
 RB = 8
 CB = 8
+
+
+def collect(x, axis, dim):
+    ways = lax.axis_size(axis)
+    up = [(d, (d + 1) % ways) for d in range(ways)]
+    down = [(d, (d - 1) % ways) for d in range(ways)]
+    earlier, later = ([x], [x])
+    for _ in range(ways // 2):
+        earlier.append(lax.ppermute(earlier[-1], axis, up))
+    for _ in range((ways - 1) // 2):
+        later.append(lax.ppermute(later[-1], axis, down))
+    line = jnp.concatenate([*earlier[::-1], *later[1:]], axis=dim)
+    return jnp.roll(line, (lax.axis_index(axis) - ways // 2) * x.shape[dim], axis=dim)
 
 
 def split_up(shard, dim, devices):
@@ -50,7 +63,7 @@
     left_table = left_home[0, 0]
     up_table = up_home[0, 0]
     left_all = lax.all_gather(left_local, "col", axis=0, tiled=True)
-    up_all = lax.all_gather(up_local, "row", axis=0, tiled=True)
+    up_all = collect(up_local, "row", 0)
     left_pairs = jnp.take(left_all, left_table, axis=0)
     up_pairs = jnp.take(up_all, up_table, axis=0)
     chosen = targets[0, 0]

time: 274 us -> 246 us (0.90); the launches traced: 273 us -> 242 us
  waiting for transfers between devices: 175 us -> 47.1 us
  starting transfers between devices: 0.08 us -> 66.1 us
  local copies, waits for them, and re-layouts: 26.7 us -> 43.1 us
  blocking collectives: 12.9 us -> 25 us
    all_gather x1, waiting for transfers between devices: 109 us -> 0.02 us  [shards(): left_all = lax.all_gather(left_local, 'col', axis=0, tiled=True)]
    ppermute x0 -> x15, starting transfers between devices: none -> 66.1 us  [the longest x7 46.5 us: collect(): later.append(lax.ppermute(later[-1], axis, down))]
    all_gather x1 -> x0, waiting for transfers between devices: 65 us -> none  [shards(): up_all = lax.all_gather(up_local, 'row', axis=0, tiled=True)]
    ppermute x0 -> x15, waiting for transfers between devices: none -> 46.4 us  [the longest x8 46.1 us: collect(): earlier.append(lax.ppermute(earlier[-1], axis, up))]
    unnamed x6 -> x45, local copies, waits for them, and re-layouts: 0.03 us -> 12.7 us
    all_to_all x2, blocking collectives: 8.78 us -> 20.9 us  [sent_and_summed(): lax.all_to_all(split_up(shard, dim, devices), axis, 0, 0, tiled=True)]
    dynamic_slice x0 -> x1, local copies, waits for them, and re-layouts: none -> 4.09 us  [collect(): jnp.roll(line, (lax.axis_index(axis) - ways // 2) * x.shape[dim], axis=dim)]
  transfers between devices with their start and end apart: 2 -> 16, of which waited for: 2 -> 9; matrix products, arithmetic and copies ran while one was open for 9% -> 19% of each run, Pallas kernels for 0% -> 0%
where the time goes in v1:
time: 246 us; the launch traced here: 242 us
  starting transfers between devices  66.1 us (27%)
  waiting for transfers between devices  47.1 us (19%)
  local copies, waits for them, and re-layouts  43.1 us (18%)
  other arithmetic  38 us (15%)
  blocking collectives  25 us (10%)
  between operations  14.6 us (6%)
  matrix products  8.32 us (3%)
    ppermute x7, starting transfers between devices, collect(): later.append(lax.ppermute(later[-1], axis, down))  46.5 us
    ppermute x8, waiting for transfers between devices, collect(): earlier.append(lax.ppermute(earlier[-1], axis, up))  46.1 us
    all_to_all x2, blocking collectives, sent_and_summed(): lax.all_to_all(split_up(shard, dim, devices), axis, 0, 0, tiled=True)  20.9 us
    ppermute x8, starting transfers between devices, collect(): earlier.append(lax.ppermute(earlier[-1], axis, up))  19.6 us
    unnamed x45, local copies, waits for them, and re-layouts  12.7 us
    select_n x2, other arithmetic, shards(): up_pairs = jnp.take(up_all, up_table, axis=0)  9.36 us
    select_n x2, other arithmetic, shards(): left_pairs = jnp.take(left_all, left_table, axis=0)  9.29 us
    gather x1, local copies, waits for them, and re-layouts, shards(): left_pairs = jnp.take(left_all, left_table, axis=0)  7.7 us
  transfers between devices with their start and end apart: 16, of which 9 were waited for; matrix products, arithmetic and copies ran while one was open for 19% of the time, Pallas kernels for 0%

profile of v1, /device:TPU:1, one launch (start us, length us, event | category | flops | bytes accessed | tf_op | source)
XLA Modules:
  0.0 242.2 jit_solution(12375369298792287076)
XLA Ops:
  7.2 0.7 all-gather.3.cloned.1.call-update
  7.9 3.9 %collective-permute-start = (f32[1,2,64,1024]{3,2,1,0:T(8,128)}, f32[1,2,64,1024]{3,2,1,0:T(8,128)S(1)}, u32[]{:S(2)}, u32[]{:S(2)}) collective-permute-start(f32[1,2,64,1024]{3,2,1,0:T(8,128)} %bitcast.99), channel_id=1, source_target_pairs={{0,32},{32,64},{64,96},{96,128},{128,160},{160,192},{192,224},{224... | collective-permute-start | bytes 1572872 | tf_op jit(solution)/shard_map/ppermute | solution.py:18
  11.9 10.5 %collective-permute-done = f32[1,2,64,1024]{3,2,1,0:T(8,128)S(1)} collective-permute-done((f32[1,2,64,1024]{3,2,1,0:T(8,128)}, f32[1,2,64,1024]{3,2,1,0:T(8,128)S(1)}, u32[]{:S(2)}, u32[]{:S(2)}) %collective-permute-start) | collective-permute-done | bytes 524320 | tf_op jit(solution)/shard_map/ppermute | solution.py:18
  22.4 3.5 %collective-permute-start.1 = (f32[1,2,64,1024]{3,2,1,0:T(8,128)S(1)}, f32[1,2,64,1024]{3,2,1,0:T(8,128)S(1)}, u32[]{:S(2)}, u32[]{:S(2)}) collective-permute-start(f32[1,2,64,1024]{3,2,1,0:T(8,128)S(1)} %collective-permute-done), channel_id=1, source_target_pairs={{0,32},{32,64},{64,96},{96,128},{128,160},{160,192},{192,224},{224... | collective-permute-start | bytes 1572872 | tf_op jit(solution)/shard_map/ppermute | solution.py:18
  25.9 6.5 %collective-permute-start.8 = (f32[1,2,64,1024]{3,2,1,0:T(8,128)}, f32[1,2,64,1024]{3,2,1,0:T(8,128)S(1)}, u32[]{:S(2)}, u32[]{:S(2)}) collective-permute-start(f32[1,2,64,1024]{3,2,1,0:T(8,128)} %bitcast.100), channel_id=1, source_target_pairs={{0,480},{32,0},{64,32},{96,64},{128,96},{160,128},{192,160},{224,1... | collective-permute-start | bytes 1572872 | tf_op jit(solution)/shard_map/ppermute | solution.py:20
  32.4 4.6 %collective-permute-done.1 = f32[1,2,64,1024]{3,2,1,0:T(8,128)S(1)} collective-permute-done((f32[1,2,64,1024]{3,2,1,0:T(8,128)S(1)}, f32[1,2,64,1024]{3,2,1,0:T(8,128)S(1)}, u32[]{:S(2)}, u32[]{:S(2)}) %collective-permute-start.1) | collective-permute-done | bytes 524320 | tf_op jit(solution)/shard_map/ppermute | solution.py:18
  37.0 2.6 %collective-permute-start.2 = (f32[1,2,64,1024]{3,2,1,0:T(8,128)S(1)}, f32[1,2,64,1024]{3,2,1,0:T(8,128)S(1)}, u32[]{:S(2)}, u32[]{:S(2)}) collective-permute-start(f32[1,2,64,1024]{3,2,1,0:T(8,128)S(1)} %collective-permute-done.1), channel_id=1, source_target_pairs={{0,32},{32,64},{64,96},{96,128},{128,160},{160,192},{192,224},{224... | collective-permute-start | bytes 1572872 | tf_op jit(solution)/shard_map/ppermute | solution.py:18
  39.6 6.7 %collective-permute-start.9 = (f32[1,2,64,1024]{3,2,1,0:T(8,128)S(1)}, f32[1,2,64,1024]{3,2,1,0:T(8,128)S(1)}, u32[]{:S(2)}, u32[]{:S(2)}) collective-permute-start(f32[1,2,64,1024]{3,2,1,0:T(8,128)S(1)} %collective-permute-done.8), channel_id=1, source_target_pairs={{0,480},{32,0},{64,32},{96,64},{128,96},{160,128},{192,160},{224,1... | collective-permute-start | bytes 1572872 | tf_op jit(solution)/shard_map/ppermute | solution.py:20
  46.4 4.6 %collective-permute-done.2 = f32[1,2,64,1024]{3,2,1,0:T(8,128)S(1)} collective-permute-done((f32[1,2,64,1024]{3,2,1,0:T(8,128)S(1)}, f32[1,2,64,1024]{3,2,1,0:T(8,128)S(1)}, u32[]{:S(2)}, u32[]{:S(2)}) %collective-permute-start.2) | collective-permute-done | bytes 524320 | tf_op jit(solution)/shard_map/ppermute | solution.py:18
  51.0 1.9 collective-permute-start.3
  52.9 6.7 %collective-permute-start.10 = (f32[1,2,64,1024]{3,2,1,0:T(8,128)S(1)}, f32[1,2,64,1024]{3,2,1,0:T(8,128)}, u32[]{:S(2)}, u32[]{:S(2)}) collective-permute-start(f32[1,2,64,1024]{3,2,1,0:T(8,128)S(1)} %collective-permute-done.9), channel_id=1, source_target_pairs={{0,480},{32,0},{64,32},{96,64},{128,96},{160,128},{192,160},{224,1... | collective-permute-start | bytes 1572872 | tf_op jit(solution)/shard_map/ppermute | solution.py:20
  59.6 4.6 %collective-permute-done.3 = f32[1,2,64,1024]{3,2,1,0:T(8,128)S(1)} collective-permute-done((f32[1,2,64,1024]{3,2,1,0:T(8,128)S(1)}, f32[1,2,64,1024]{3,2,1,0:T(8,128)S(1)}, u32[]{:S(2)}, u32[]{:S(2)}) %collective-permute-start.3) | collective-permute-done | bytes 524320 | tf_op jit(solution)/shard_map/ppermute | solution.py:18
  64.2 1.9 collective-permute-start.4
  66.4 6.6 %collective-permute-start.11 = (f32[1,2,64,1024]{3,2,1,0:T(8,128)}, f32[1,2,64,1024]{3,2,1,0:T(8,128)}, u32[]{:S(2)}, u32[]{:S(2)}) collective-permute-start(f32[1,2,64,1024]{3,2,1,0:T(8,128)} %collective-permute-done.10), channel_id=1, source_target_pairs={{0,480},{32,0},{64,32},{96,64},{128,96},{160,128},{192,160},{224,1... | collective-permute-start | bytes 1572872 | tf_op jit(solution)/shard_map/ppermute | solution.py:20
  73.0 4.6 %collective-permute-done.4 = f32[1,2,64,1024]{3,2,1,0:T(8,128)} collective-permute-done((f32[1,2,64,1024]{3,2,1,0:T(8,128)S(1)}, f32[1,2,64,1024]{3,2,1,0:T(8,128)}, u32[]{:S(2)}, u32[]{:S(2)}) %collective-permute-start.4) | collective-permute-done | bytes 524320 | tf_op jit(solution)/shard_map/ppermute | solution.py:18
  77.6 1.9 collective-permute-start.5
  79.5 0.7 compare_select_fusion.3
  80.3 6.7 %collective-permute-start.12 = (f32[1,2,64,1024]{3,2,1,0:T(8,128)}, f32[1,2,64,1024]{3,2,1,0:T(8,128)S(1)}, u32[]{:S(2)}, u32[]{:S(2)}) collective-permute-start(f32[1,2,64,1024]{3,2,1,0:T(8,128)} %collective-permute-done.11), channel_id=1, source_target_pairs={{0,480},{32,0},{64,32},{96,64},{128,96},{160,128},{192,160},{224,1... | collective-permute-start | bytes 1572872 | tf_op jit(solution)/shard_map/ppermute | solution.py:20
  87.0 5.0 %collective-permute-done.5 = f32[1,2,64,1024]{3,2,1,0:T(8,128)} collective-permute-done((f32[1,2,64,1024]{3,2,1,0:T(8,128)}, f32[1,2,64,1024]{3,2,1,0:T(8,128)}, u32[]{:S(2)}, u32[]{:S(2)}) %collective-permute-start.5) | collective-permute-done | bytes 524320 | tf_op jit(solution)/shard_map/ppermute | solution.py:18
  91.9 1.9 collective-permute-start.6
  93.9 0.7 compare_and_fusion
  94.5 0.7 compare_select_fusion.1
  95.2 6.7 %collective-permute-start.13 = (f32[1,2,64,1024]{3,2,1,0:T(8,128)S(1)}, f32[1,2,64,1024]{3,2,1,0:T(8,128)S(1)}, u32[]{:S(2)}, u32[]{:S(2)}) collective-permute-start(f32[1,2,64,1024]{3,2,1,0:T(8,128)S(1)} %collective-permute-done.12), channel_id=1, source_target_pairs={{0,480},{32,0},{64,32},{96,64},{128,96},{160,128},{192,160},{224,1... | collective-permute-start | bytes 1572872 | tf_op jit(solution)/shard_map/ppermute | solution.py:20
  101.9 5.5 %collective-permute-done.6 = f32[1,2,64,1024]{3,2,1,0:T(8,128)S(1)} collective-permute-done((f32[1,2,64,1024]{3,2,1,0:T(8,128)}, f32[1,2,64,1024]{3,2,1,0:T(8,128)S(1)}, u32[]{:S(2)}, u32[]{:S(2)}) %collective-permute-start.6) | collective-permute-done | bytes 524320 | tf_op jit(solution)/shard_map/ppermute | solution.py:18
  107.4 1.9 collective-permute-start.7
  109.3 0.7 compare_and_fusion.3
  110.0 0.7 compare_and_fusion.1
  110.6 6.7 %collective-permute-start.14 = (f32[1,2,64,1024]{3,2,1,0:T(8,128)S(1)}, f32[1,2,64,1024]{3,2,1,0:T(8,128)S(1)}, u32[]{:S(2)}, u32[]{:S(2)}) collective-permute-start(f32[1,2,64,1024]{3,2,1,0:T(8,128)S(1)} %collective-permute-done.13), channel_id=1, source_target_pairs={{0,480},{32,0},{64,32},{96,64},{128,96},{160,128},{192,160},{224,1... | collective-permute-start | bytes 1572872 | tf_op jit(solution)/shard_map/ppermute | solution.py:20
  117.3 6.7 %collective-permute-done.7 = f32[1,2,64,1024]{3,2,1,0:T(8,128)S(1)} collective-permute-done((f32[1,2,64,1024]{3,2,1,0:T(8,128)S(1)}, f32[1,2,64,1024]{3,2,1,0:T(8,128)S(1)}, u32[]{:S(2)}, u32[]{:S(2)}) %collective-permute-start.7) | collective-permute-done | bytes 524320 | tf_op jit(solution)/shard_map/ppermute | solution.py:18
  124.1 1.1 constant_dynamic-update-slice_fusion.29
  125.2 1.1 constant_dynamic-update-slice_fusion.28
  126.3 1.1 constant_dynamic-update-slice_fusion.27
  127.4 1.1 constant_dynamic-update-slice_fusion.26
  128.5 1.1 constant_dynamic-update-slice_fusion.23
  129.7 1.1 constant_dynamic-update-slice_fusion.20
  130.8 1.1 constant_dynamic-update-slice_fusion.19
  132.1 1.1 constant_dynamic-update-slice_fusion.13
  133.2 1.1 constant_dynamic-update-slice_fusion.12
  134.6 1.1 constant_dynamic-update-slice_fusion.4
  135.7 1.1 constant_dynamic-update-slice_fusion.3
  137.0 4.1 %constant_dynamic-slice_fusion = f32[16,2,64,1024]{3,2,1,0:T(8,128)} fusion(f32[32,2,64,1024]{3,2,1,0:T(8,128)S(1)} %constant_dynamic-update-slice_fusion, s32[]{:T(128)S(6)} %select_n.42), kind=kLoop, calls=%fused_computation.81 | loop fusion | bytes 16777220 | tf_op jit(solution)/shard_map/jit(_roll_dynamic)/dynamic_slice | solution.py:22
  141.0 7.7 %gather_fusion = f32[16,2,64,1024]{3,2,1,0:T(8,128)} fusion(f32[16,2,64,1024]{3,2,1,0:T(8,128)} %constant_dynamic-slice_fusion, s32[1024]{0:T(1024)S(1)} %pad_clamp_fusion.3), kind=kCustom, calls=%fused_computation.clone | custom fusion | bytes 16777280 | tf_op jit(solution)/shard_map/jit(_take)/gather | solution.py:68
  148.7 8.6 %broadcast_select_fusion.1 = f32[16,2,64,1024]{3,2,1,0:T(8,128)} fusion(f32[16,2,64,1024]{3,2,1,0:T(8,128)} %gather_fusion, pred[16]{0:T(512)(128)(4,1)S(1)} %compare_and_fusion.3), kind=kLoop, calls=%fused_computation.5 | loop fusion | flops 2097152 | bytes 16777232 | tf_op jit(solution)/shard_map/jit(_take)/select_n | solution.py:68
  157.3 5.4 %gather_fusion.1 = f32[2,2,2,64,1024]{4,3,2,1,0:T(8,128)} fusion(f32[8,2,2,64,1024]{4,3,2,1,0:T(8,128)} %bitcast.97, s32[1024]{0:T(1024)S(1)} %get-tuple-element.11), kind=kCustom, calls=%fused_computation.1.clone | custom fusion | bytes 4194312 | tf_op jit(solution)/shard_map/jit(_take)/gather | solution.py:73
  162.8 1.9 copy_select_fusion.1
  164.7 1.6 fusion.1
  166.3 7.7 %gather_fusion.2 = f32[16,2,64,1024]{3,2,1,0:T(8,128)} fusion(f32[16,2,64,1024]{3,2,1,0:T(8,128)} %bitcast.98, s32[1024]{0:T(1024)S(1)} %pad_clamp_fusion.1), kind=kCustom, calls=%fused_computation.2.clone | custom fusion | bytes 16777280 | tf_op jit(solution)/shard_map/jit(_take)/gather | solution.py:67
  174.0 8.6 %broadcast_select_fusion = f32[16,2,64,1024]{3,2,1,0:T(8,128)} fusion(f32[16,2,64,1024]{3,2,1,0:T(8,128)} %gather_fusion.2, pred[16]{0:T(512)(128)(4,1)S(1)} %compare_and_fusion.1), kind=kLoop, calls=%fused_computation.4 | loop fusion | flops 2097152 | bytes 16777232 | tf_op jit(solution)/shard_map/jit(_take)/select_n | solution.py:67
  182.6 5.4 %gather_fusion.3 = f32[2,2,2,64,1024]{4,3,2,1,0:T(8,128)} fusion(f32[8,2,2,64,1024]{4,3,2,1,0:T(8,128)} %bitcast.96, s32[1024]{0:T(1024)S(1)} %get-tuple-element.10), kind=kCustom, calls=%fused_computation.3.clone | custom fusion | bytes 4194312 | tf_op jit(solution)/shard_map/jit(_take)/gather | solution.py:72
  188.0 1.9 copy_select_fusion
  189.9 1.1 fusion
  191.4 0.7 convolution_bitcast_fusion.1
  192.1 16.7 %all_to_all.15 = f32[2,1,64,1024]{3,2,1,0:T(8,128)S(1)} all-to-all(f32[2,1,64,1024]{3,2,1,0:T(8,128)S(1)} %convolution_bitcast_fusion.1), channel_id=1, replica_groups=mesh['row'=16,'col'=16,'depth'=2] {'depth'}, dimensions={0} | all-to-all | bytes 1048576 | tf_op jit(solution)/shard_map/all_to_all | solution.py:32
  209.3 5.8 %custom-call.7 = f32[1,64,64]{2,1,0:T(8,128)S(1)} custom-call(f32[1,64,64]{2,1,0:T(8,128)S(1)} %fusion.6), custom_call_target="Cholesky" | custom-call | tf_op jit(solution)/shard_map/jit(cholesky)/cholesky | solution.py:55
  215.2 0.6 compare_reduce_fusion
  215.8 0.7 fusion.5
  216.5 4.9 %custom-call.8 = f32[1,1,64,64]{2,3,1,0:T(8,128)S(1)} custom-call(f32[1,1,64,64]{3,2,1,0:T(8,128)S(1)} %fusion.5), custom_call_target="InvertDiagBlocksLowerTriangular" | custom-call | tf_op jit(solution)/shard_map/triangular_solve | solution.py:56
  221.4 0.4 fusion.7
  221.8 0.7 multiply_bitcast_fusion.1
  222.6 4.1 %all_to_all.16 = f32[2,1,64,1024]{3,2,1,0:T(8,128)S(1)} all-to-all(f32[2,1,64,1024]{3,2,1,0:T(8,128)S(1)} %broadcast_in_dim.33), channel_id=1, replica_groups=mesh['row'=16,'col'=16,'depth'=2] {'depth'}, dimensions={0} | all-to-all | bytes 1048576 | tf_op jit(solution)/shard_map/all_to_all | solution.py:44
  226.7 2.8 %fusion.2 = f32[2,2,64,64]{2,3,1,0:T(8,128)S(1)} fusion(f32[2,2,2,64,1024]{4,3,1,0,2:T(8,128)} %copy-done.1, f32[2,1,64,1024]{3,2,1,0:T(8,128)S(1)} %all_to_all.16), kind=kOutput, calls=%fused_computation.16 | convolution fusion | flops 201326592 | bytes 1638400 | tf_op jit(solution)/shard_map/pat,pkct->pkac/dot_general | solution.py:86
  229.8 0.7 convolution_bitcast_fusion
  230.5 4.2 %all_to_all.17 = f32[2,1,64,1024]{3,2,1,0:T(8,128)S(1)} all-to-all(f32[2,1,64,1024]{3,2,1,0:T(8,128)S(1)} %convolution_bitcast_fusion), channel_id=1, replica_groups=mesh['row'=16,'col'=16,'depth'=2] {'depth'}, dimensions={0} | all-to-all | bytes 1048576 | tf_op jit(solution)/shard_map/all_to_all | solution.py:32
  234.7 0.7 multiply_bitcast_fusion
  (56 shorter events, 2.3 us)
Async XLA Ops:
  7.2 157.5 %copy-start = (f32[1,1,2,64,1024]{4,3,2,1,0:T(8,128)S(1)}, f32[1,1,2,64,1024]{4,3,2,1,0:T(8,128)}, u32[]{:S(2)}) copy-start(f32[1,1,2,64,1024]{4,3,2,1,0:T(8,128)} %param.15) | copy-start | bytes 1572868
  7.2 127.3 %copy-start.2 = (f32[1,1,1,2,64,1024]{5,4,3,2,1,0:T(8,128)S(1)}, f32[1,1,1,2,64,1024]{5,4,3,2,1,0:T(8,128)}, u32[]{:S(2)}) copy-start(f32[1,1,1,2,64,1024]{5,4,3,2,1,0:T(8,128)} %param.12) | copy-start | bytes 1572868
  7.2 159.1 %all-gather.3.cloned.1.call-start = ((), (), s32[]{:S(2)}) async-start(), calls=%async_computation.3 | async-start | bytes 8912896 | tf_op jit(solution)/shard_map/all_gather | solution.py:65
  7.9 14.4 %collective-permute-start = (f32[1,2,64,1024]{3,2,1,0:T(8,128)}, f32[1,2,64,1024]{3,2,1,0:T(8,128)S(1)}, u32[]{:S(2)}, u32[]{:S(2)}) collective-permute-start(f32[1,2,64,1024]{3,2,1,0:T(8,128)} %bitcast.99), channel_id=1, source_target_pairs={{0,32},{32,64},{64,96},{96,128},{128,160},{160,192},{192,224},{224... | collective-permute-start | bytes 1572872 | tf_op jit(solution)/shard_map/ppermute | solution.py:18
  22.4 14.7 %collective-permute-start.1 = (f32[1,2,64,1024]{3,2,1,0:T(8,128)S(1)}, f32[1,2,64,1024]{3,2,1,0:T(8,128)S(1)}, u32[]{:S(2)}, u32[]{:S(2)}) collective-permute-start(f32[1,2,64,1024]{3,2,1,0:T(8,128)S(1)} %collective-permute-done), channel_id=1, source_target_pairs={{0,32},{32,64},{64,96},{96,128},{128,160},{160,192},{192,224},{224... | collective-permute-start | bytes 1572872 | tf_op jit(solution)/shard_map/ppermute | solution.py:18
  25.9 13.7 %collective-permute-start.8 = (f32[1,2,64,1024]{3,2,1,0:T(8,128)}, f32[1,2,64,1024]{3,2,1,0:T(8,128)S(1)}, u32[]{:S(2)}, u32[]{:S(2)}) collective-permute-start(f32[1,2,64,1024]{3,2,1,0:T(8,128)} %bitcast.100), channel_id=1, source_target_pairs={{0,480},{32,0},{64,32},{96,64},{128,96},{160,128},{192,160},{224,1... | collective-permute-start | bytes 1572872 | tf_op jit(solution)/shard_map/ppermute | solution.py:20
  37.0 13.9 %collective-permute-start.2 = (f32[1,2,64,1024]{3,2,1,0:T(8,128)S(1)}, f32[1,2,64,1024]{3,2,1,0:T(8,128)S(1)}, u32[]{:S(2)}, u32[]{:S(2)}) collective-permute-start(f32[1,2,64,1024]{3,2,1,0:T(8,128)S(1)} %collective-permute-done.1), channel_id=1, source_target_pairs={{0,32},{32,64},{64,96},{96,128},{128,160},{160,192},{192,224},{224... | collective-permute-start | bytes 1572872 | tf_op jit(solution)/shard_map/ppermute | solution.py:18
  39.6 13.3 %collective-permute-start.9 = (f32[1,2,64,1024]{3,2,1,0:T(8,128)S(1)}, f32[1,2,64,1024]{3,2,1,0:T(8,128)S(1)}, u32[]{:S(2)}, u32[]{:S(2)}) collective-permute-start(f32[1,2,64,1024]{3,2,1,0:T(8,128)S(1)} %collective-permute-done.8), channel_id=1, source_target_pairs={{0,480},{32,0},{64,32},{96,64},{128,96},{160,128},{192,160},{224,1... | collective-permute-start | bytes 1572872 | tf_op jit(solution)/shard_map/ppermute | solution.py:20
  51.0 15.4 %copy-start.3 = (f32[1,2,64,1024]{3,2,1,0:T(8,128)}, f32[1,2,64,1024]{3,2,1,0:T(8,128)S(1)}, u32[]{:S(2)}) copy-start(f32[1,2,64,1024]{3,2,1,0:T(8,128)S(1)} %collective-permute-done.2) | copy-start | bytes 1572868
  51.0 13.2 %collective-permute-start.3 = (f32[1,2,64,1024]{3,2,1,0:T(8,128)S(1)}, f32[1,2,64,1024]{3,2,1,0:T(8,128)S(1)}, u32[]{:S(2)}, u32[]{:S(2)}) collective-permute-start(f32[1,2,64,1024]{3,2,1,0:T(8,128)S(1)} %collective-permute-done.2), channel_id=1, source_target_pairs={{0,32},{32,64},{64,96},{96,128},{128,160},{160,192},{192,224},{224... | collective-permute-start | bytes 1572872 | tf_op jit(solution)/shard_map/ppermute | solution.py:18
  52.9 13.5 %collective-permute-start.10 = (f32[1,2,64,1024]{3,2,1,0:T(8,128)S(1)}, f32[1,2,64,1024]{3,2,1,0:T(8,128)}, u32[]{:S(2)}, u32[]{:S(2)}) collective-permute-start(f32[1,2,64,1024]{3,2,1,0:T(8,128)S(1)} %collective-permute-done.9), channel_id=1, source_target_pairs={{0,480},{32,0},{64,32},{96,64},{128,96},{160,128},{192,160},{224,1... | collective-permute-start | bytes 1572872 | tf_op jit(solution)/shard_map/ppermute | solution.py:20
  64.2 8.7 %copy-start.5 = (f32[1,2,64,1024]{3,2,1,0:T(8,128)}, f32[1,2,64,1024]{3,2,1,0:T(8,128)S(1)}, u32[]{:S(2)}) copy-start(f32[1,2,64,1024]{3,2,1,0:T(8,128)S(1)} %collective-permute-done.3) | copy-start | bytes 1572868
  64.2 13.3 %collective-permute-start.4 = (f32[1,2,64,1024]{3,2,1,0:T(8,128)S(1)}, f32[1,2,64,1024]{3,2,1,0:T(8,128)}, u32[]{:S(2)}, u32[]{:S(2)}) collective-permute-start(f32[1,2,64,1024]{3,2,1,0:T(8,128)S(1)} %collective-permute-done.3), channel_id=1, source_target_pairs={{0,32},{32,64},{64,96},{96,128},{128,160},{160,192},{192,224},{224... | collective-permute-start | bytes 1572872 | tf_op jit(solution)/shard_map/ppermute | solution.py:18
  66.4 13.9 %collective-permute-start.11 = (f32[1,2,64,1024]{3,2,1,0:T(8,128)}, f32[1,2,64,1024]{3,2,1,0:T(8,128)}, u32[]{:S(2)}, u32[]{:S(2)}) collective-permute-start(f32[1,2,64,1024]{3,2,1,0:T(8,128)} %collective-permute-done.10), channel_id=1, source_target_pairs={{0,480},{32,0},{64,32},{96,64},{128,96},{160,128},{192,160},{224,1... | collective-permute-start | bytes 1572872 | tf_op jit(solution)/shard_map/ppermute | solution.py:20
  77.6 14.4 %collective-permute-start.5 = (f32[1,2,64,1024]{3,2,1,0:T(8,128)}, f32[1,2,64,1024]{3,2,1,0:T(8,128)}, u32[]{:S(2)}, u32[]{:S(2)}) collective-permute-start(f32[1,2,64,1024]{3,2,1,0:T(8,128)} %collective-permute-done.4), channel_id=1, source_target_pairs={{0,32},{32,64},{64,96},{96,128},{128,160},{160,192},{192,224},{224... | collective-permute-start | bytes 1572872 | tf_op jit(solution)/shard_map/ppermute | solution.py:18
  79.5 54.8 %copy-start.6 = (f32[1,2,64,1024]{3,2,1,0:T(8,128)S(1)}, f32[1,2,64,1024]{3,2,1,0:T(8,128)}, u32[]{:S(2)}) copy-start(f32[1,2,64,1024]{3,2,1,0:T(8,128)} %copy-done.5) | copy-start | bytes 1572868
  79.5 54.8 %copy-start.4 = (f32[1,2,64,1024]{3,2,1,0:T(8,128)S(1)}, f32[1,2,64,1024]{3,2,1,0:T(8,128)}, u32[]{:S(2)}) copy-start(f32[1,2,64,1024]{3,2,1,0:T(8,128)} %copy-done.3) | copy-start | bytes 1572868
  80.3 14.9 %collective-permute-start.12 = (f32[1,2,64,1024]{3,2,1,0:T(8,128)}, f32[1,2,64,1024]{3,2,1,0:T(8,128)S(1)}, u32[]{:S(2)}, u32[]{:S(2)}) collective-permute-start(f32[1,2,64,1024]{3,2,1,0:T(8,128)} %collective-permute-done.11), channel_id=1, source_target_pairs={{0,480},{32,0},{64,32},{96,64},{128,96},{160,128},{192,160},{224,1... | collective-permute-start | bytes 1572872 | tf_op jit(solution)/shard_map/ppermute | solution.py:20
  91.9 15.4 %collective-permute-start.6 = (f32[1,2,64,1024]{3,2,1,0:T(8,128)}, f32[1,2,64,1024]{3,2,1,0:T(8,128)S(1)}, u32[]{:S(2)}, u32[]{:S(2)}) collective-permute-start(f32[1,2,64,1024]{3,2,1,0:T(8,128)} %collective-permute-done.5), channel_id=1, source_target_pairs={{0,32},{32,64},{64,96},{96,128},{128,160},{160,192},{192,224},{224... | collective-permute-start | bytes 1572872 | tf_op jit(solution)/shard_map/ppermute | solution.py:18
  95.2 15.4 %collective-permute-start.13 = (f32[1,2,64,1024]{3,2,1,0:T(8,128)S(1)}, f32[1,2,64,1024]{3,2,1,0:T(8,128)S(1)}, u32[]{:S(2)}, u32[]{:S(2)}) collective-permute-start(f32[1,2,64,1024]{3,2,1,0:T(8,128)S(1)} %collective-permute-done.12), channel_id=1, source_target_pairs={{0,480},{32,0},{64,32},{96,64},{128,96},{160,128},{192,160},{224,1... | collective-permute-start | bytes 1572872 | tf_op jit(solution)/shard_map/ppermute | solution.py:20
  107.4 16.7 %collective-permute-start.7 = (f32[1,2,64,1024]{3,2,1,0:T(8,128)S(1)}, f32[1,2,64,1024]{3,2,1,0:T(8,128)S(1)}, u32[]{:S(2)}, u32[]{:S(2)}) collective-permute-start(f32[1,2,64,1024]{3,2,1,0:T(8,128)S(1)} %collective-permute-done.6), channel_id=1, source_target_pairs={{0,32},{32,64},{64,96},{96,128},{128,160},{160,192},{192,224},{224... | collective-permute-start | bytes 1572872 | tf_op jit(solution)/shard_map/ppermute | solution.py:18
  110.6 21.4 %collective-permute-start.14 = (f32[1,2,64,1024]{3,2,1,0:T(8,128)S(1)}, f32[1,2,64,1024]{3,2,1,0:T(8,128)S(1)}, u32[]{:S(2)}, u32[]{:S(2)}) collective-permute-start(f32[1,2,64,1024]{3,2,1,0:T(8,128)S(1)} %collective-permute-done.13), channel_id=1, source_target_pairs={{0,480},{32,0},{64,32},{96,64},{128,96},{160,128},{192,160},{224,1... | collective-permute-start | bytes 1572872 | tf_op jit(solution)/shard_map/ppermute | solution.py:20
  189.9 1.5 copy-start.1
Sparse Core Ops, SparseCore 0:
  10.1 110.9 all-gather.2
